TPU v7x, 32 devices: a whole 2x2x4 slice. The times are simulated.
32 devices in a mesh: gx: 2 (over core), gy: 4 (over y, x), ga: 4 (over z).
Axes of the slice: x: 2, y: 2, z: 4, core: 2. Of those that a mesh axis runs over, the one named last changes fastest.
Arguments:
- concentration: float32 [12, 128, 2048], P(None, 'gx', ('gy', 'ga')), may hold values from 0 to 2
- velocity: float32 [2, 128, 2048], P(None, 'gx', ('gy', 'ga')), may hold values from -0.4 to 0.4, as said below
- solid_fraction: float32 [128, 2048], P('gx', ('gy', 'ga')), may hold values from 0 to 1
- diffusivity: float32 [12], replicated, may hold values from 0.02 to 0.1
- voxel_index: int32 [32, 2048], P(('gx', 'gy', 'ga')), may hold values from 0 to 8191, as said below
- voxel_counts: int32 [2, 16], P('gx'), may hold values from 1 to 2048, 8192 in all within a row
- in_weight: bfloat16 [13, 128], replicated, may hold values from -1.75 to 1.75
- in_bias: float32 [128], replicated, may hold values from -3 to 3
- mid_weight: bfloat16 [128, 128], replicated, may hold values from -0.5 to 0.5
- mid_bias: float32 [128], replicated, may hold values from -3 to 3
- out_weight: bfloat16 [128, 12], replicated, may hold values from -0.5 to 0.5
- out_bias: float32 [12], replicated, may hold values from -2 to 2
Outputs:
- final_concentration: float32 [12, 128, 2048], P(None, 'gx', ('gy', 'ga'))
Inputs may be any that keep to these rules, and one draw needn't show every extreme that they name: velocity[0] lies in -0.4 to 0.4 and velocity[1] in -0.15 to 0.15. `voxel_index`: each row holds 2048 different cells of its tile, as flat indices row * 128 + column. `voxel_counts`: in each row the 16 counts sum to 8192, and the largest is 2048.
All inputs are finite; a program needn't handle non-finite values.
Results may differ from a plain program's by a relative error of at most 0.00067.
Values may be sent and summed in bfloat16 or wider, within the bound.
A program may use at most 64 MiB of HBM per device.

v0:
```python
import jax
import jax.numpy as jnp
from jax import lax
from jax.sharding import PartitionSpec as P

SUBSTEPS = 4
COUPLINGS = 16
VOX_CAP = 2048


def extended(block, sides, width):
    for axis, dim in sides:
        count = lax.axis_size(axis)
        forward = [(i, i + 1) for i in range(count - 1)]
        backward = [(target, source) for source, target in forward]
        low = lax.ppermute(
            lax.slice_in_dim(block, block.shape[dim] - width, None, axis=dim), axis, forward
        )
        high = lax.ppermute(lax.slice_in_dim(block, 0, width, axis=dim), axis, backward)
        block = jnp.concatenate([low, block, high], axis=dim)
    return block


def advance(padded, velocity, diffusivity):
    centre = padded[:, 1:-1, 1:-1]
    above_rows = padded[:, :-2, 1:-1]
    below_rows = padded[:, 2:, 1:-1]
    left_cols = padded[:, 1:-1, :-2]
    right_cols = padded[:, 1:-1, 2:]
    speed_rows = velocity[0]
    speed_cols = velocity[1]
    upwind = jnp.maximum(speed_rows, 0.0) * (centre - above_rows) + jnp.minimum(speed_rows, 0.0) * (
        below_rows - centre
    )
    upwind = (
        upwind
        + jnp.maximum(speed_cols, 0.0) * (centre - left_cols)
        + jnp.minimum(speed_cols, 0.0) * (right_cols - centre)
    )
    mixing = diffusivity[:, None, None] * (
        above_rows + below_rows + (left_cols + right_cols) - 4.0 * centre
    )
    return centre - upwind + mixing


def surrogate_cells(features, weights):
    in_weight, in_bias, mid_weight, mid_bias, out_weight, out_bias = weights
    layer_one = jnp.einsum("ir,ih->hr", features, in_weight, preferred_element_type=jnp.float32)
    layer_one = jnp.tanh(layer_one + in_bias[:, None]).astype(jnp.bfloat16)
    layer_two = jnp.einsum("hr,hk->kr", layer_one, mid_weight, preferred_element_type=jnp.float32)
    layer_two = jnp.tanh(layer_two + mid_bias[:, None]).astype(jnp.bfloat16)
    output = jnp.einsum("kr,ks->sr", layer_two, out_weight, preferred_element_type=jnp.float32)
    return (output + out_bias[:, None]).astype(jnp.bfloat16)


def per_device(
    concentration,
    velocity,
    solid_fraction,
    diffusivity,
    voxel_index,
    voxel_counts,
    in_weight,
    in_bias,
    mid_weight,
    mid_bias,
    out_weight,
    out_bias,
):
    weights = (in_weight, in_bias, mid_weight, mid_bias, out_weight, out_bias)
    species = concentration.shape[0]
    rows_local = concentration.shape[1]
    cols_local = concentration.shape[2]
    voxel_list = voxel_index[0]
    counts_row = voxel_counts[0]
    own_count = counts_row[lax.axis_index(("gy", "ga"))]
    live_mask = jnp.arange(VOX_CAP, dtype=jnp.int32) < own_count
    solid_cells = solid_fraction.reshape(-1)[voxel_list]

    def transport(solutes):
        for substep in range(SUBSTEPS):
            padded = extended(solutes, (("gx", 1), (("gy", "ga"), 2)), 1)
            solutes = advance(padded, velocity, diffusivity)
        return solutes

    def coupling(counter, solutes):
        solutes = transport(solutes)
        flat_field = solutes.reshape(species, rows_local * cols_local)
        gathered = jnp.concatenate(
            [flat_field[:, voxel_list], solid_cells[None, :]], axis=0
        ).astype(jnp.bfloat16)
        increment = surrogate_cells(gathered, weights)
        increment = lax.optimization_barrier(increment).astype(jnp.float32)
        increment = jnp.where(live_mask[None, :], increment, 0.0)
        flat_field = flat_field.at[:, voxel_list].add(increment)
        return flat_field.reshape(species, rows_local, cols_local)

    return lax.fori_loop(0, COUPLINGS, coupling, concentration)


def solution(mesh):
    return jax.shard_map(
        per_device,
        mesh=mesh,
        in_specs=(
            P(None, "gx", ("gy", "ga")),
            P(None, "gx", ("gy", "ga")),
            P("gx", ("gy", "ga")),
            P(),
            P(("gx", "gy", "ga"), None),
            P("gx", None),
            P(),
            P(),
            P(),
            P(),
            P(),
            P(),
        ),
        out_specs=P(None, "gx", ("gy", "ga")),
        check_vma=False,
    )
```

profile of v0, /device:TPU:5, one launch (start us, length us, event | category | flops | bytes accessed | tf_op | source)
XLA Modules:
  0.0 2267.0 jit_solution(9383021380291510512)
XLA Ops:
  2.1 11.6 gather_fusion.1
  16.6 2246.9 %while.12 = (s32[]{:T(128)}, f32[12,64,128]{0,2,1:T(8,128)}, f32[2,64,128]{2,1,0:T(8,128)S(1)}, f32[12]{0:T(128)S(1)}, s32[2048]{0:T(1024)S(1)}, /*index=5*/bf16...) while((s32[]{:T(128)}, f32[12,64,128]{0,2,1:T(8,128)}, ...), condition=%wide.wide.region_2.3_spmd.clone, body=%wide.wide.region_0.2_spmd.clone.sunk | while | flops 92964864 | bytes 11294209 | solution.py:98
  40.9 10.3 collective-permute-done.3
  72.5 10.4 collective-permute-done.7
  151.9 14.5 scatter_fusion
  208.8 8.5 collective-permute-done.6
  291.7 14.5 scatter_fusion
  348.6 8.5 collective-permute-done.6
  431.6 14.5 scatter_fusion
  488.4 8.5 collective-permute-done.6
  571.4 14.5 scatter_fusion
  628.3 8.5 collective-permute-done.6
  711.2 14.5 scatter_fusion
  768.1 8.5 collective-permute-done.6
  851.0 14.5 scatter_fusion
  907.9 8.5 collective-permute-done.6
  990.8 14.5 scatter_fusion
  1047.7 8.5 collective-permute-done.6
  1130.6 14.5 scatter_fusion
  1187.5 8.5 collective-permute-done.6
  1270.4 14.5 scatter_fusion
  1410.2 14.5 scatter_fusion
  1467.1 8.5 collective-permute-done.6
  1550.0 14.5 scatter_fusion
  1606.9 8.5 collective-permute-done.6
  1689.8 14.5 scatter_fusion
  1746.7 8.5 collective-permute-done.6
  1829.6 14.5 scatter_fusion
  1969.4 14.5 scatter_fusion
  2109.2 14.5 scatter_fusion
  2166.1 8.5 collective-permute-done.6
  2249.0 14.5 scatter_fusion
  (989 shorter events, 1895.8 us)
Async XLA Ops:
  31.5 19.8 collective-permute-start.3
  63.0 19.9 collective-permute-start.7
  91.6 19.8 collective-permute-start.11
  120.1 19.2 collective-permute-start.15
  204.7 19.2 collective-permute-start.7
  232.3 19.2 collective-permute-start.11
  344.5 19.2 collective-permute-start.7
  399.8 19.2 collective-permute-start.15
  484.3 19.2 collective-permute-start.7
  539.6 19.2 collective-permute-start.15
  596.5 19.2 collective-permute-start.3
  624.1 19.2 collective-permute-start.7
  651.8 19.2 collective-permute-start.11
  736.3 19.2 collective-permute-start.3
  791.6 19.2 collective-permute-start.11
  876.1 19.2 collective-permute-start.3
  931.4 19.2 collective-permute-start.11
  959.0 19.2 collective-permute-start.15
  1043.6 19.2 collective-permute-start.7
  1098.8 19.2 collective-permute-start.15
  1183.4 19.2 collective-permute-start.7
  1238.6 19.2 collective-permute-start.15
  1295.6 19.2 collective-permute-start.3
  1323.2 19.2 collective-permute-start.7
  1350.8 19.2 collective-permute-start.11
  1435.4 19.2 collective-permute-start.3
  1490.6 19.2 collective-permute-start.11
  1575.2 19.2 collective-permute-start.3
  1630.4 19.2 collective-permute-start.11
  1658.0 19.2 collective-permute-start.15
  1742.6 19.2 collective-permute-start.7
  1797.8 19.2 collective-permute-start.15
  (235 other events, 2136.4 us)
where the time goes:
time: 2280 us; the launch traced here: 2270 us
  waiting for transfers between devices  1080 us (47%)
  starting transfers between devices  634 us (28%)
  other arithmetic  281 us (12%)
  local copies, waits for them, and re-layouts  255 us (11%)
    ppermute x128, waiting for transfers between devices, extended(): lax.ppermute(lax.slice_in_dim(block, block.shape[dim] - width, None, axis...  544 us
    ppermute x128, waiting for transfers between devices, extended(): lax.ppermute(lax.slice_in_dim(block, 0, width, axis=dim), axis, backward)  533 us
    ppermute x128, starting transfers between devices, extended(): lax.ppermute(lax.slice_in_dim(block, block.shape[dim] - width, None, axis...  340 us
    ppermute x128, starting transfers between devices, extended(): lax.ppermute(lax.slice_in_dim(block, 0, width, axis=dim), axis, backward)  295 us
    scatter-add x16, other arithmetic, coupling(): flat_field = flat_field.at[:, voxel_list].add(increment)  231 us
    gather x16, local copies, waits for them, and re-layouts, coupling(): flat_field[:, voxel_list]  124 us
    while x16, local copies, waits for them, and re-layouts  46.2 us
  transfers between devices with their start and end apart: 256, of which 192 were waited for; matrix products, arithmetic and copies ran while one was open for 0% of the time, Pallas kernels for 0%

commit v1 on v0

v1 whole, which is shorter than its diff:
```python
import jax
import jax.numpy as jnp
from jax import lax
from jax.experimental import pallas as pl
from jax.experimental.pallas import tpu as pltpu
from jax.sharding import PartitionSpec as P

SUBSTEPS = 4
COUPLINGS = 16
HALO = SUBSTEPS
SLOTS = 16
CHUNK = 8
MESH = pl.DeviceIdType.MESH


def kernel(
    rows, cols, species, gx_count, gy_count, ga_count,
    base_ref, vel_ref, diff_ref, index_ref, counts_ref, w1_ref, w2_ref, w3_ref,
    out_ref,
    state, other, coef_c, coef_u, coef_d, coef_l, coef_r, live,
    edge_out, top_out, bottom_out,
    from_left, from_right, from_up, from_down, from_corner,
    send_sem, recv_sem,
):
    full = rows + 2 * HALO
    width = 2 * HALO
    per_tile = cols // width
    tiles = rows // per_tile
    gx = lax.axis_index("gx")
    gy = lax.axis_index("gy")
    ga = lax.axis_index("ga")
    place = gy * ga_count + ga
    places = gy_count * ga_count

    def device(dx, dp):
        other_place = jnp.clip(place + dp, 0, places - 1)
        return (
            jnp.clip(gx + dx, 0, gx_count - 1),
            lax.div(other_place, ga_count),
            lax.rem(other_place, ga_count),
        )

    has_up, has_down = gx > 0, gx < gx_count - 1
    has_left, has_right = place > 0, place < places - 1
    links = (
        (device(0, -1), has_left),
        (device(0, 1), has_right),
        (device(-1, 0), has_up),
        (device(1, 0), has_down),
        (device(-1, -1), has_up & has_left),
        (device(1, 1), has_down & has_right),
        (device(-1, 1), has_up & has_right),
        (device(1, -1), has_down & has_left),
    )

    for ref in (from_left, from_right, from_up, from_down, from_corner):
        ref[...] = jnp.zeros_like(ref)

    barrier = pltpu.get_barrier_semaphore()
    total = jnp.int32(0)
    for target, exists in links:
        total = total + exists.astype(jnp.int32)

        @pl.when(exists)
        def _():
            pl.semaphore_signal(barrier, inc=1, device_id=target, device_id_type=MESH)

    pl.semaphore_wait(barrier, total)

    lane = lax.broadcasted_iota(jnp.int32, (SLOTS, cols), 1)
    sub = lax.broadcasted_iota(jnp.int32, (SLOTS, cols), 0)
    first_half = lax.rem(lane, width) < HALO

    def copies(slot):
        last = tiles - 1
        plan = (
            (edge_out, from_right.at[slot]),
            (edge_out, from_left.at[slot]),
            (top_out, from_down.at[slot]),
            (bottom_out, from_up.at[slot]),
            (edge_out.at[0], from_corner.at[slot, 3]),
            (edge_out.at[last], from_corner.at[slot, 0]),
            (edge_out.at[0], from_corner.at[slot, 2]),
            (edge_out.at[last], from_corner.at[slot, 1]),
        )
        result = []
        for at, ((source, target_ref), (target, exists)) in enumerate(zip(plan, links)):
            result.append((
                pltpu.make_async_remote_copy(
                    src_ref=source, dst_ref=target_ref,
                    send_sem=send_sem.at[at], recv_sem=recv_sem.at[slot, at],
                    device_id=target, device_id_type=MESH,
                ),
                exists,
            ))
        return result

    def start(slot):
        for tile in range(tiles):
            packed = jnp.zeros((SLOTS, cols), jnp.float32)
            for at in range(per_tile):
                row = state[HALO + tile * per_tile + at, :, 0:cols]
                moved = pltpu.roll(row, (width * at + HALO) % cols, axis=1)
                packed = moved if at == 0 else jnp.where(lane >= width * at, moved, packed)
            edge_out[tile] = packed
        top_out[...] = state[HALO : 2 * HALO, :, 0:cols]
        bottom_out[...] = state[rows : rows + HALO, :, 0:cols]
        for copy, exists in copies(slot):

            @pl.when(exists)
            def _():
                copy.start()

    def finish(slot, change):
        moves = copies(slot)
        for at, (copy, exists) in enumerate(moves):

            @pl.when(exists)
            def _():
                copy.wait_send()

            @pl.when(links[at ^ 1][1])
            def _():
                moves[at][0].wait_recv()

        edges = [
            jnp.where(first_half, from_left[slot, tile], from_right[slot, tile])
            for tile in range(tiles)
        ]
        corner_up = jnp.where(first_half, from_corner[slot, 0], from_corner[slot, 1])
        corner_down = jnp.where(first_half, from_corner[slot, 2], from_corner[slot, 3])
        corner = jnp.where(lane < width * HALO, corner_down, corner_up)
        blocks = edges + [corner]
        blocks += [from_up[slot, at] for at in range(HALO)]
        blocks += [from_down[slot, at] for at in range(HALO)]
        if change is not None:
            blocks = change(blocks)
        corner = blocks[tiles]
        for at in range(HALO):
            state[at, :, 0:cols] = blocks[tiles + 1 + at]
            state[HALO + rows + at, :, 0:cols] = blocks[tiles + 1 + HALO + at]
            window = per_tile - HALO + at
            state[at, :, cols : 2 * cols] = pltpu.roll(
                corner, (2 * cols - width * window - HALO) % cols, axis=1
            )
            state[HALO + rows + at, :, cols : 2 * cols] = pltpu.roll(
                corner, (2 * cols - width * at - HALO) % cols, axis=1
            )
        for tile in range(tiles):
            for at in range(per_tile):
                state[HALO + tile * per_tile + at, :, cols : 2 * cols] = pltpu.roll(
                    blocks[tile], (2 * cols - width * at - HALO) % cols, axis=1
                )

    def react(blocks):
        count = len(blocks)
        features = jnp.concatenate([block.astype(jnp.bfloat16) for block in blocks], axis=1)
        ones = jnp.ones((SLOTS, count * cols), jnp.bfloat16)
        hidden = jnp.dot(w1_ref[...], features, preferred_element_type=jnp.float32)
        hidden = jnp.tanh(hidden).astype(jnp.bfloat16)
        hidden = jnp.concatenate([hidden, ones], axis=0)
        hidden = jnp.dot(w2_ref[...], hidden, preferred_element_type=jnp.float32)
        hidden = jnp.tanh(hidden).astype(jnp.bfloat16)
        hidden = jnp.concatenate([hidden, ones], axis=0)
        gain = jnp.dot(w3_ref[...], hidden, preferred_element_type=jnp.float32)
        gain = gain.astype(jnp.bfloat16).astype(jnp.float32)
        return [
            block
            + jnp.where(
                jnp.broadcast_to(block[species + 1 : species + 2], block.shape) > 0.5,
                gain[:, at * cols : (at + 1) * cols],
                0.0,
            )
            for at, block in enumerate(blocks)
        ]

    @pl.loop(0, rows)
    def _(row):
        speed_rows = jnp.broadcast_to(vel_ref[0, pl.ds(row, 1), :], (SLOTS, cols))
        speed_cols = jnp.broadcast_to(vel_ref[1, pl.ds(row, 1), :], (SLOTS, cols))
        state[HALO + row, :, 0:cols] = jnp.where(
            sub == 0, speed_rows, jnp.where(sub == 1, speed_cols, 1.0)
        )

    start(0)

    candidates = index_ref[...]
    counts = counts_ref[...]
    own = lax.broadcasted_iota(jnp.int32, counts.shape, 1) == place
    own_count = jnp.sum(jnp.where(own, counts, 0), axis=1, keepdims=True)
    entry = lax.broadcasted_iota(jnp.int32, candidates.shape, 1)
    candidates = jnp.where(entry < own_count, candidates, -1)
    cell_row = jnp.right_shift(candidates, cols.bit_length() - 1)
    cell_col = jnp.bitwise_and(candidates, cols - 1)
    entries = candidates.shape[1]
    row_at = lax.broadcasted_iota(jnp.int32, (rows, entries), 0)
    col_at = lax.broadcasted_iota(jnp.int32, (cols, entries), 0)
    row_hot = jnp.where(row_at == cell_row, 1.0, 0.0).astype(jnp.bfloat16)
    col_hot = jnp.where(col_at == cell_col, 1.0, 0.0).astype(jnp.bfloat16)
    live[...] = lax.dot_general(
        row_hot, col_hot, (((1,), (1,)), ((), ())), preferred_element_type=jnp.float32
    )

    finish(0, None)
    sub2 = lax.broadcasted_iota(jnp.int32, (SLOTS, 2 * cols), 0)
    shares = diff_ref[...]
    spread = jnp.broadcast_to(shares, (SLOTS, 2 * cols))

    @pl.loop(0, full)
    def _(row):
        block = state[row]
        inside = jnp.where(sub2 < species, jnp.broadcast_to(block[2:3], block.shape), 0.0)
        speed_rows = jnp.broadcast_to(block[0:1], block.shape)
        speed_cols = jnp.broadcast_to(block[1:2], block.shape)
        coef_u[row] = inside * (jnp.maximum(speed_rows, 0.0) + spread)
        coef_d[row] = inside * (spread - jnp.minimum(speed_rows, 0.0))
        coef_l[row] = inside * (jnp.maximum(speed_cols, 0.0) + spread)
        coef_r[row] = inside * (spread - jnp.minimum(speed_cols, 0.0))
        coef_c[row] = 1.0 - inside * (
            jnp.abs(speed_rows) + jnp.abs(speed_cols) + 4.0 * spread
        )

    @pl.loop(0, rows)
    def _(row):
        flags = jnp.broadcast_to(live[pl.ds(row, 1), :], (SLOTS, cols))
        state[HALO + row, :, 0:cols] = jnp.where(sub == species + 1, flags, base_ref[row])

    start(1)
    finish(1, None)

    def substep(source, target, low, high):
        def body(row, carry):
            above, centre = carry
            below = source[row + 1]
            target[row] = (
                coef_c[row] * centre
                + coef_u[row] * above
                + coef_d[row] * below
                + coef_l[row] * pltpu.roll(centre, 1, axis=1)
                + coef_r[row] * pltpu.roll(centre, 2 * cols - 1, axis=1)
            )
            return centre, below

        lax.fori_loop(low, high, body, (source[low - 1], source[low]), unroll=2)

    @pl.loop(0, COUPLINGS)
    def _(step):
        for at in range(SUBSTEPS):
            source, target = (state, other) if at % 2 == 0 else (other, state)
            substep(source, target, at + 1, full - 1 - at)
        slot = lax.rem(step, 2)
        start(slot)

        @pl.loop(0, rows // CHUNK)
        def _(piece):
            first = HALO + piece * CHUNK
            blocks = react([state[first + at, :, 0:cols] for at in range(CHUNK)])
            for at in range(CHUNK):
                state[first + at, :, 0:cols] = blocks[at]

        finish(slot, react)

    out_ref[...] = state[HALO : HALO + rows, :, 0:cols]


def split_bias(bias):
    high = lax.reduce_precision(bias, 8, 7)
    return jnp.stack([high, bias - high], axis=1).astype(jnp.bfloat16)


def per_device(
    concentration, velocity, solid_fraction, diffusivity, voxel_index, voxel_counts,
    in_weight, in_bias, mid_weight, mid_bias, out_weight, out_bias,
):
    species, rows, cols = concentration.shape
    hidden = mid_weight.shape[0]
    base = jnp.concatenate(
        [
            jnp.transpose(concentration, (1, 0, 2)),
            solid_fraction[:, None, :],
            jnp.zeros((rows, 1, cols), jnp.float32),
            jnp.ones((rows, SLOTS - species - 2, cols), jnp.float32),
        ],
        axis=1,
    )
    shares = jnp.pad(diffusivity, (0, SLOTS - species))[:, None]
    w1 = jnp.concatenate(
        [in_weight.T, jnp.zeros((hidden, 1), jnp.bfloat16), split_bias(in_bias)], axis=1
    )
    gap = jnp.zeros((hidden, SLOTS - 2), jnp.bfloat16)
    w2 = jnp.concatenate([mid_weight.T, split_bias(mid_bias), gap], axis=1)
    w3 = jnp.concatenate([out_weight.T, split_bias(out_bias), gap[:species]], axis=1)
    w3 = jnp.pad(w3, ((0, SLOTS - species), (0, 0)))
    full = rows + 2 * HALO
    tiles = rows * 2 * HALO // cols
    sizes = [lax.axis_size(name) for name in ("gx", "gy", "ga")]

    def body(*refs):
        kernel(rows, cols, species, *sizes, *refs)

    whole = pltpu.VMEM((full, SLOTS, 2 * cols), jnp.float32)
    result = pl.pallas_call(
        body,
        out_shape=jax.ShapeDtypeStruct((rows, SLOTS, cols), jnp.float32),
        in_specs=[pl.BlockSpec(memory_space=pltpu.VMEM)] * 8,
        out_specs=pl.BlockSpec(memory_space=pltpu.VMEM),
        scratch_shapes=[whole] * 7
        + [
            pltpu.VMEM((rows, cols), jnp.float32),
            pltpu.VMEM((tiles, SLOTS, cols), jnp.float32),
            pltpu.VMEM((HALO, SLOTS, cols), jnp.float32),
            pltpu.VMEM((HALO, SLOTS, cols), jnp.float32),
            pltpu.VMEM((2, tiles, SLOTS, cols), jnp.float32),
            pltpu.VMEM((2, tiles, SLOTS, cols), jnp.float32),
            pltpu.VMEM((2, HALO, SLOTS, cols), jnp.float32),
            pltpu.VMEM((2, HALO, SLOTS, cols), jnp.float32),
            pltpu.VMEM((2, 4, SLOTS, cols), jnp.float32),
            pltpu.SemaphoreType.DMA((8,)),
            pltpu.SemaphoreType.DMA((2, 8)),
        ],
        compiler_params=pltpu.CompilerParams(
            collective_id=0, has_side_effects=True, vmem_limit_bytes=48 << 20
        ),
    )(base, velocity, shares, voxel_index, voxel_counts, w1, w2, w3)
    return jnp.transpose(result[:, :species, :], (1, 0, 2))


def solution(mesh):
    tile = P(None, "gx", ("gy", "ga"))
    return jax.shard_map(
        per_device,
        mesh=mesh,
        in_specs=(
            tile, tile, P("gx", ("gy", "ga")), P(),
            P(("gx", "gy", "ga"), None), P("gx", None),
            P(), P(), P(), P(), P(), P(),
        ),
        out_specs=tile,
        check_vma=False,
    )
```

time: 2280 us -> 311 us (0.14)
  waiting for transfers between devices: 1080 us -> 0 us
  starting transfers between devices: 634 us -> 0 us
  Pallas kernels: 0 us -> 302 us
  other arithmetic: 281 us -> 3.79 us
  local copies, waits for them, and re-layouts: 255 us -> 4.5 us
    ppermute x256 -> x0, waiting for transfers between devices: 1080 us -> none  [the longest x128 544 us: extended(): lax.ppermute(lax.slice_in_dim(block, block.shape[dim] - width, None, axis...]
    ppermute x256 -> x0, starting transfers between devices: 634 us -> none  [the longest x128 340 us: extended(): lax.ppermute(lax.slice_in_dim(block, block.shape[dim] - width, None, axis...]
    pallas_call x0 -> x1, Pallas kernels: none -> 302 us  [per_device(): pl.pallas_call(body, out_shape=jax.ShapeDtypeStruct((rows, SLOTS, cols),...]
    scatter-add x16 -> x0, other arithmetic: 231 us -> none  [coupling(): flat_field = flat_field.at[:, voxel_list].add(increment)]
    gather x17 -> x0, local copies, waits for them, and re-layouts: 136 us -> none  [the longest x16 124 us: coupling(): flat_field[:, voxel_list]]
    while x17 -> x0, local copies, waits for them, and re-layouts: 49.7 us -> none
    add x16 -> x0, local copies, waits for them, and re-layouts: 43.2 us -> none  [advance(): return centre - upwind + mixing]
    add x64 -> x0, other arithmetic: 36 us -> none  [advance(): return centre - upwind + mixing]
  transfers between devices with their start and end apart: 256 -> 0, of which waited for: 192 -> 0; matrix products, arithmetic and copies ran while one was open for 0% -> 0% of each run, Pallas kernels for 0% -> 0%
where the time goes in v1:
time: 311 us; the launch traced here: 310 us
  Pallas kernels  302 us (97%)
  local copies, waits for them, and re-layouts  4.5 us (1%)
  other arithmetic  3.79 us (1%)
    pallas_call x1, Pallas kernels, per_device(): pl.pallas_call(body, out_shape=jax.ShapeDtypeStruct((rows, SLOTS, cols),...  302 us

profile of v1, /device:TPU:5, one launch (start us, length us, event | category | flops | bytes accessed | tf_op | source)
XLA Modules:
  0.0 310.2 jit_solution(10358710672099113797)
XLA Ops:
  0.0 0.0 copy-start.3
  0.0 0.7 fusion.3
  0.7 0.1 copy.26
  0.9 0.1 copy.27
  1.0 0.1 pad.17.clone
  1.1 0.9 copy.25
  1.9 0.1 maximum_maximum_fusion.1.refs_6_
  2.0 0.7 fusion.6
  2.7 0.1 copy.28
  2.8 0.1 copy.29
  2.9 0.8 maximum_maximum_fusion.2
  3.7 0.7 fusion
  4.4 0.1 pad.19.clone
  4.4 0.8 pad_maximum_fusion
  5.2 0.1 copy.31.refs_5_
  5.3 0.0 copy-done.3
  5.3 0.0 copy-start.4
  5.3 0.2 copy.34
  5.6 0.1 pad.25.clone
  5.7 0.1 pad.24.clone
  5.7 0.3 copy-done.4
  6.1 0.0 copy-start
  6.1 0.1 maximum_maximum_fusion.refs_0_
  6.2 0.5 copy-done.5
  6.7 0.0 copy-start.1
  6.7 0.0 copy-start.2
  6.7 0.1 copy.30.refs_2_
  6.8 0.1 copy-done
  6.9 0.5 copy-done.1
  7.4 0.0 copy-done.2
  7.4 301.9 %shard_map.118 = f32[64,16,128]{2,1,0:T(8,128)S(1)} custom-call(f32[64,16,128]{2,1,0:T(8,128)S(1)} %maximum_maximum_fusion.refs_0_, f32[2,64,128]{2,1,0:T(8,128)S(1)} %copy-done, f32[16,1]{1,0:T(8,128)S(1)} %copy.30.refs_2_, s32[1,2048]{1,0:T(1,128)S(1)} %copy-done.1, s32[1,16]{1,0:T(1,128)S(1)} %copy-done.2, bf16[128,16]{1,0:T(8,128)(2,1)S(1)} %copy.31.refs_5_, ...), custom_call_target="tpu_custom_call" | custom-call | tf_op jit(solution)/shard_map/pallas_call | solution.py:302
  309.4 0.9 copy.32
  (6 shorter events, 0.1 us)
Async XLA Ops:
  0.0 5.3 %copy-start.3 = (f32[12,64,128]{2,1,0:T(8,128)S(1)}, f32[12,64,128]{2,1,0:T(8,128)}, u32[]{:S(2)}) copy-start(f32[12,64,128]{2,1,0:T(8,128)} %param.12) | copy-start | bytes 1179652
  5.3 0.8 copy-start.4
  6.1 0.7 copy-start.5
  6.1 0.9 copy-start
  6.7 0.7 copy-start.1
  6.7 0.7 copy-start.2

commit v2 on v1

--- a/solution.py
+++ b/solution.py
@@ -10,6 +10,7 @@
 HALO = SUBSTEPS
 SLOTS = 16
 CHUNK = 8
+GROUP = 10
 MESH = pl.DeviceIdType.MESH
 
 
@@ -225,29 +226,29 @@
         flags = jnp.broadcast_to(live[pl.ds(row, 1), :], (SLOTS, cols))
         state[HALO + row, :, 0:cols] = jnp.where(sub == species + 1, flags, base_ref[row])
 
+    other[...] = jnp.zeros_like(other)
     start(1)
     finish(1, None)
 
-    def substep(source, target, low, high):
-        def body(row, carry):
-            above, centre = carry
-            below = source[row + 1]
-            target[row] = (
-                coef_c[row] * centre
-                + coef_u[row] * above
-                + coef_d[row] * below
-                + coef_l[row] * pltpu.roll(centre, 1, axis=1)
-                + coef_r[row] * pltpu.roll(centre, 2 * cols - 1, axis=1)
+    def substep(source, target):
+        @pl.loop(0, (full - 2) // GROUP)
+        def _(group):
+            row = 1 + group * GROUP
+            here = pl.ds(row, GROUP)
+            centre = source[here]
+            target[here] = (
+                coef_c[here] * centre
+                + coef_u[here] * source[pl.ds(row - 1, GROUP)]
+                + coef_d[here] * source[pl.ds(row + 1, GROUP)]
+                + coef_l[here] * pltpu.roll(centre, 1, axis=2)
+                + coef_r[here] * pltpu.roll(centre, 2 * cols - 1, axis=2)
             )
-            return centre, below
-
-        lax.fori_loop(low, high, body, (source[low - 1], source[low]), unroll=2)
 
     @pl.loop(0, COUPLINGS)
     def _(step):
         for at in range(SUBSTEPS):
             source, target = (state, other) if at % 2 == 0 else (other, state)
-            substep(source, target, at + 1, full - 1 - at)
+            substep(source, target)
         slot = lax.rem(step, 2)
         start(slot)
 

time: 311 us -> 200 us (0.64)
  Pallas kernels: 302 us -> 191 us
    pallas_call x1, Pallas kernels: 302 us -> 191 us  [per_device(): pl.pallas_call(body, out_shape=jax.ShapeDtypeStruct((rows, SLOTS, cols),...]
where the time goes in v2:
time: 200 us; the launch traced here: 199 us
  Pallas kernels  191 us (96%)
  local copies, waits for them, and re-layouts  4.5 us (2%)
  other arithmetic  3.79 us (2%)
    pallas_call x1, Pallas kernels, per_device(): pl.pallas_call(body, out_shape=jax.ShapeDtypeStruct((rows, SLOTS, cols),...  191 us

profile of v2, /device:TPU:5, one launch (start us, length us, event | category | flops | bytes accessed | tf_op | source)
XLA Modules:
  0.0 199.4 jit_solution(10759217447862755956)
XLA Ops:
  0.0 0.0 copy-start.3
  0.0 0.7 fusion.3
  0.7 0.1 copy.26
  0.9 0.1 copy.27
  1.0 0.1 pad.17.clone
  1.1 0.9 copy.25
  1.9 0.1 maximum_maximum_fusion.1.refs_6_
  2.0 0.7 fusion.6
  2.7 0.1 copy.28
  2.8 0.1 copy.29
  2.9 0.8 maximum_maximum_fusion.2
  3.7 0.7 fusion
  4.4 0.1 pad.19.clone
  4.4 0.8 pad_maximum_fusion
  5.2 0.1 copy.31.refs_5_
  5.3 0.0 copy-done.3
  5.3 0.0 copy-start.4
  5.3 0.2 copy.34
  5.6 0.1 pad.25.clone
  5.7 0.1 pad.24.clone
  5.7 0.3 copy-done.4
  6.1 0.0 copy-start
  6.1 0.1 maximum_maximum_fusion.refs_0_
  6.2 0.5 copy-done.5
  6.7 0.0 copy-start.1
  6.7 0.0 copy-start.2
  6.7 0.1 copy.30.refs_2_
  6.8 0.1 copy-done
  6.9 0.5 copy-done.1
  7.4 0.0 copy-done.2
  7.4 191.1 %shard_map.118 = f32[64,16,128]{2,1,0:T(8,128)S(1)} custom-call(f32[64,16,128]{2,1,0:T(8,128)S(1)} %maximum_maximum_fusion.refs_0_, f32[2,64,128]{2,1,0:T(8,128)S(1)} %copy-done, f32[16,1]{1,0:T(8,128)S(1)} %copy.30.refs_2_, s32[1,2048]{1,0:T(1,128)S(1)} %copy-done.1, s32[1,16]{1,0:T(1,128)S(1)} %copy-done.2, bf16[128,16]{1,0:T(8,128)(2,1)S(1)} %copy.31.refs_5_, ...), custom_call_target="tpu_custom_call" | custom-call | tf_op jit(solution)/shard_map/pallas_call | solution.py:303
  198.6 0.9 copy.32
  (6 shorter events, 0.1 us)
Async XLA Ops:
  0.0 5.3 %copy-start.3 = (f32[12,64,128]{2,1,0:T(8,128)S(1)}, f32[12,64,128]{2,1,0:T(8,128)}, u32[]{:S(2)}) copy-start(f32[12,64,128]{2,1,0:T(8,128)} %param.12) | copy-start | bytes 1179652
  5.3 0.8 copy-start.4
  6.1 0.7 copy-start.5
  6.1 0.9 copy-start
  6.7 0.7 copy-start.1
  6.7 0.7 copy-start.2

commit v3 on v2

--- a/solution.py
+++ b/solution.py
@@ -10,7 +10,7 @@
 HALO = SUBSTEPS
 SLOTS = 16
 CHUNK = 8
-GROUP = 10
+GROUP = 70
 MESH = pl.DeviceIdType.MESH
 
 
@@ -168,22 +168,12 @@
         return [
             block
             + jnp.where(
-                jnp.broadcast_to(block[species + 1 : species + 2], block.shape) > 0.5,
+                jnp.broadcast_to(block[species + 1 : species + 2], block.shape) > 1.5,
                 gain[:, at * cols : (at + 1) * cols],
                 0.0,
             )
             for at, block in enumerate(blocks)
         ]
-
-    @pl.loop(0, rows)
-    def _(row):
-        speed_rows = jnp.broadcast_to(vel_ref[0, pl.ds(row, 1), :], (SLOTS, cols))
-        speed_cols = jnp.broadcast_to(vel_ref[1, pl.ds(row, 1), :], (SLOTS, cols))
-        state[HALO + row, :, 0:cols] = jnp.where(
-            sub == 0, speed_rows, jnp.where(sub == 1, speed_cols, 1.0)
-        )
-
-    start(0)
 
     candidates = index_ref[...]
     counts = counts_ref[...]
@@ -202,17 +192,28 @@
         row_hot, col_hot, (((1,), (1,)), ((), ())), preferred_element_type=jnp.float32
     )
 
+    @pl.loop(0, rows)
+    def _(row):
+        flags = 1.0 + jnp.broadcast_to(live[pl.ds(row, 1), :], (SLOTS, cols))
+        speed_rows = jnp.broadcast_to(vel_ref[0, pl.ds(row, 1), :], (SLOTS, cols))
+        speed_cols = jnp.broadcast_to(vel_ref[1, pl.ds(row, 1), :], (SLOTS, cols))
+        block = jnp.where(sub == species + 1, flags, base_ref[row])
+        block = jnp.where(sub == species + 2, speed_rows, block)
+        state[HALO + row, :, 0:cols] = jnp.where(sub == species + 3, speed_cols, block)
+
+    start(0)
+    other[...] = jnp.zeros_like(other)
     finish(0, None)
     sub2 = lax.broadcasted_iota(jnp.int32, (SLOTS, 2 * cols), 0)
-    shares = diff_ref[...]
-    spread = jnp.broadcast_to(shares, (SLOTS, 2 * cols))
+    spread = jnp.broadcast_to(diff_ref[...], (SLOTS, 2 * cols))
 
     @pl.loop(0, full)
     def _(row):
         block = state[row]
-        inside = jnp.where(sub2 < species, jnp.broadcast_to(block[2:3], block.shape), 0.0)
-        speed_rows = jnp.broadcast_to(block[0:1], block.shape)
-        speed_cols = jnp.broadcast_to(block[1:2], block.shape)
+        inside = jnp.minimum(jnp.broadcast_to(block[species + 1 : species + 2], block.shape), 1.0)
+        inside = jnp.where(sub2 < species, inside, 0.0)
+        speed_rows = jnp.broadcast_to(block[species + 2 : species + 3], block.shape)
+        speed_cols = jnp.broadcast_to(block[species + 3 : species + 4], block.shape)
         coef_u[row] = inside * (jnp.maximum(speed_rows, 0.0) + spread)
         coef_d[row] = inside * (spread - jnp.minimum(speed_rows, 0.0))
         coef_l[row] = inside * (jnp.maximum(speed_cols, 0.0) + spread)
@@ -220,15 +221,7 @@
         coef_c[row] = 1.0 - inside * (
             jnp.abs(speed_rows) + jnp.abs(speed_cols) + 4.0 * spread
         )
-
-    @pl.loop(0, rows)
-    def _(row):
-        flags = jnp.broadcast_to(live[pl.ds(row, 1), :], (SLOTS, cols))
-        state[HALO + row, :, 0:cols] = jnp.where(sub == species + 1, flags, base_ref[row])
-
-    other[...] = jnp.zeros_like(other)
-    start(1)
-    finish(1, None)
+        state[row] = jnp.where(sub2 < species + 2, block, 1.0)
 
     def substep(source, target):
         @pl.loop(0, (full - 2) // GROUP)
@@ -249,8 +242,11 @@
         for at in range(SUBSTEPS):
             source, target = (state, other) if at % 2 == 0 else (other, state)
             substep(source, target)
-        slot = lax.rem(step, 2)
-        start(slot)
+        slot = lax.rem(step + 1, 2)
+
+        @pl.when(step < COUPLINGS - 1)
+        def _():
+            start(slot)
 
         @pl.loop(0, rows // CHUNK)
         def _(piece):
@@ -259,7 +255,9 @@
             for at in range(CHUNK):
                 state[first + at, :, 0:cols] = blocks[at]
 
-        finish(slot, react)
+        @pl.when(step < COUPLINGS - 1)
+        def _():
+            finish(slot, react)
 
     out_ref[...] = state[HALO : HALO + rows, :, 0:cols]
 

time: 200 us -> 173 us (0.86)
  Pallas kernels: 191 us -> 165 us
    pallas_call x1, Pallas kernels: 191 us -> 165 us  [per_device(): pl.pallas_call(body, out_shape=jax.ShapeDtypeStruct((rows, SLOTS, cols),...]
where the time goes in v3:
time: 173 us
  Pallas kernels  165 us (95%)
  local copies, waits for them, and re-layouts  4.5 us (3%)
  other arithmetic  3.79 us (2%)
    pallas_call x1, Pallas kernels, per_device(): pl.pallas_call(body, out_shape=jax.ShapeDtypeStruct((rows, SLOTS, cols),...  165 us

profile of v3, /device:TPU:5, one launch (start us, length us, event | category | flops | bytes accessed | tf_op | source)
XLA Modules:
  0.0 173.0 jit_solution(6520487771642795756)
XLA Ops:
  0.0 0.0 copy-start.3
  0.0 0.7 fusion.3
  0.7 0.1 copy.26
  0.9 0.1 copy.27
  1.0 0.1 pad.17.clone
  1.1 0.9 copy.25
  1.9 0.1 maximum_maximum_fusion.1.refs_6_
  2.0 0.7 fusion.6
  2.7 0.1 copy.28
  2.8 0.1 copy.29
  2.9 0.8 maximum_maximum_fusion.2
  3.7 0.7 fusion
  4.4 0.1 pad.19.clone
  4.4 0.8 pad_maximum_fusion
  5.2 0.1 copy.31.refs_5_
  5.3 0.0 copy-done.3
  5.3 0.0 copy-start.4
  5.3 0.2 copy.34
  5.6 0.1 pad.25.clone
  5.7 0.1 pad.24.clone
  5.7 0.3 copy-done.4
  6.1 0.0 copy-start.5
  6.1 0.0 copy-start
  6.1 0.1 maximum_maximum_fusion.refs_0_
  6.2 0.5 copy-done.5
  6.7 0.0 copy-start.2
  6.7 0.1 copy.30.refs_2_
  6.8 0.1 copy-done
  6.9 0.5 copy-done.1
  7.4 0.0 copy-done.2
  7.4 164.6 %shard_map.118 = f32[64,16,128]{2,1,0:T(8,128)S(1)} custom-call(f32[64,16,128]{2,1,0:T(8,128)S(1)} %maximum_maximum_fusion.refs_0_, f32[2,64,128]{2,1,0:T(8,128)S(1)} %copy-done, f32[16,1]{1,0:T(8,128)S(1)} %copy.30.refs_2_, s32[1,2048]{1,0:T(1,128)S(1)} %copy-done.1, s32[1,16]{1,0:T(1,128)S(1)} %copy-done.2, bf16[128,16]{1,0:T(8,128)(2,1)S(1)} %copy.31.refs_5_, ...), custom_call_target="tpu_custom_call" | custom-call | tf_op jit(solution)/shard_map/pallas_call | solution.py:301
  172.1 0.9 copy.32
  (6 shorter events, 0.1 us)
Async XLA Ops:
  0.0 5.3 %copy-start.3 = (f32[12,64,128]{2,1,0:T(8,128)S(1)}, f32[12,64,128]{2,1,0:T(8,128)}, u32[]{:S(2)}) copy-start(f32[12,64,128]{2,1,0:T(8,128)} %param.12) | copy-start | bytes 1179652
  5.3 0.8 copy-start.4
  6.1 0.7 copy-start.5
  6.1 0.9 copy-start
  6.7 0.7 copy-start.1
  6.7 0.7 copy-start.2

commit v4 on v3

--- a/solution.py
+++ b/solution.py
@@ -10,7 +10,6 @@
 HALO = SUBSTEPS
 SLOTS = 16
 CHUNK = 8
-GROUP = 70
 MESH = pl.DeviceIdType.MESH
 
 
@@ -202,7 +201,6 @@
         state[HALO + row, :, 0:cols] = jnp.where(sub == species + 3, speed_cols, block)
 
     start(0)
-    other[...] = jnp.zeros_like(other)
     finish(0, None)
     sub2 = lax.broadcasted_iota(jnp.int32, (SLOTS, 2 * cols), 0)
     spread = jnp.broadcast_to(diff_ref[...], (SLOTS, 2 * cols))
@@ -223,25 +221,22 @@
         )
         state[row] = jnp.where(sub2 < species + 2, block, 1.0)
 
-    def substep(source, target):
-        @pl.loop(0, (full - 2) // GROUP)
-        def _(group):
-            row = 1 + group * GROUP
-            here = pl.ds(row, GROUP)
-            centre = source[here]
-            target[here] = (
-                coef_c[here] * centre
-                + coef_u[here] * source[pl.ds(row - 1, GROUP)]
-                + coef_d[here] * source[pl.ds(row + 1, GROUP)]
-                + coef_l[here] * pltpu.roll(centre, 1, axis=2)
-                + coef_r[here] * pltpu.roll(centre, 2 * cols - 1, axis=2)
-            )
+    def substep(source, target, low, high):
+        here = pl.ds(low, high - low)
+        centre = source[here]
+        target[here] = (
+            coef_c[here] * centre
+            + coef_u[here] * source[pl.ds(low - 1, high - low)]
+            + coef_d[here] * source[pl.ds(low + 1, high - low)]
+            + coef_l[here] * pltpu.roll(centre, 1, axis=2)
+            + coef_r[here] * pltpu.roll(centre, 2 * cols - 1, axis=2)
+        )
 
     @pl.loop(0, COUPLINGS)
     def _(step):
         for at in range(SUBSTEPS):
             source, target = (state, other) if at % 2 == 0 else (other, state)
-            substep(source, target)
+            substep(source, target, at + 1, full - 1 - at)
         slot = lax.rem(step + 1, 2)
 
         @pl.when(step < COUPLINGS - 1)

time: 173 us -> 170 us (0.983)
  Pallas kernels: 165 us -> 161 us
    pallas_call x1, Pallas kernels: 165 us -> 161 us  [per_device(): pl.pallas_call(body, out_shape=jax.ShapeDtypeStruct((rows, SLOTS, cols),...]
where the time goes in v4:
time: 170 us; the launch traced here: 169 us
  Pallas kernels  161 us (95%)
  local copies, waits for them, and re-layouts  4.5 us (3%)
  other arithmetic  3.79 us (2%)
    pallas_call x1, Pallas kernels, per_device(): pl.pallas_call(body, out_shape=jax.ShapeDtypeStruct((rows, SLOTS, cols),...  161 us

profile of v4, /device:TPU:5, one launch (start us, length us, event | category | flops | bytes accessed | tf_op | source)
XLA Modules:
  0.0 169.2 jit_solution(13267069057911258627)
XLA Ops:
  0.0 0.0 copy-start.3
  0.0 0.7 fusion.3
  0.7 0.1 copy.26
  0.9 0.1 copy.27
  1.0 0.1 pad.17.clone
  1.1 0.9 copy.25
  1.9 0.1 maximum_maximum_fusion.1.refs_6_
  2.0 0.7 fusion.6
  2.7 0.1 copy.28
  2.8 0.1 copy.29
  2.9 0.8 maximum_maximum_fusion.2
  3.7 0.7 fusion
  4.4 0.1 pad.19.clone
  4.4 0.8 pad_maximum_fusion
  5.2 0.1 copy.31.refs_5_
  5.3 0.0 copy-done.3
  5.3 0.0 copy-start.4
  5.3 0.2 copy.34
  5.6 0.1 pad.25.clone
  5.7 0.1 pad.24.clone
  5.7 0.3 copy-done.4
  6.1 0.0 copy-start.5
  6.1 0.0 copy-start
  6.1 0.1 maximum_maximum_fusion.refs_0_
  6.2 0.5 copy-done.5
  6.7 0.0 copy-start.2
  6.7 0.1 copy.30.refs_2_
  6.8 0.1 copy-done
  6.9 0.5 copy-done.1
  7.4 0.0 copy-done.2
  7.4 160.8 %shard_map.118 = f32[64,16,128]{2,1,0:T(8,128)S(1)} custom-call(f32[64,16,128]{2,1,0:T(8,128)S(1)} %maximum_maximum_fusion.refs_0_, f32[2,64,128]{2,1,0:T(8,128)S(1)} %copy-done, f32[16,1]{1,0:T(8,128)S(1)} %copy.30.refs_2_, s32[1,2048]{1,0:T(1,128)S(1)} %copy-done.1, s32[1,16]{1,0:T(1,128)S(1)} %copy-done.2, bf16[128,16]{1,0:T(8,128)(2,1)S(1)} %copy.31.refs_5_, ...), custom_call_target="tpu_custom_call" | custom-call | tf_op jit(solution)/shard_map/pallas_call | solution.py:296
  168.3 0.9 copy.32
  (6 shorter events, 0.1 us)
Async XLA Ops:
  0.0 5.3 %copy-start.3 = (f32[12,64,128]{2,1,0:T(8,128)S(1)}, f32[12,64,128]{2,1,0:T(8,128)}, u32[]{:S(2)}) copy-start(f32[12,64,128]{2,1,0:T(8,128)} %param.12) | copy-start | bytes 1179652
  5.3 0.8 copy-start.4
  6.1 0.7 copy-start.5
  6.1 0.9 copy-start
  6.7 0.7 copy-start.1
  6.7 0.7 copy-start.2
